TPU v7x, 32 devices: a whole 2x2x4 slice. The times are simulated.
32 devices in a mesh: leaf: 8 (over z, core), sub: 4 (over y, x).
Axes of the slice: x: 2, y: 2, z: 4, core: 2. Of those that a mesh axis runs over, the one named last changes fastest.
Arguments:
- leaf_maps: float32 [32, 256, 1024], P('leaf', 'sub'), may hold values from -8 to 28, as said below
- order_one: int32 [8, 4], replicated, may hold values from 0 to 3, each once within a row
- order_two: int32 [4, 6], replicated, may hold values from 0 to 5, each once within a row
- top_data: float32 [16, 256, 256], P('leaf', 'sub'), may hold values from -6 to 6
Outputs:
- top_map: float32 [16, 256, 2048], P('leaf', 'sub')
- leaf_data: float32 [32, 256, 256], P('leaf', 'sub')
Inputs may be any that keep to these rules, and one draw needn't show every extreme that they name: Each leaf's block of 1024 rows of leaf_maps, read as a 1024 by 1024 matrix, is symmetric and positive definite.
All inputs are finite; a program needn't handle non-finite values. Where the computation divides by a largest or mean magnitude, that divisor is 1e-20 or more.
Results may differ from a plain program's by a relative error of at most 0.0001.
Values sent between devices are 32-bit elements; how exact they have to be, the bound alone decides.
No kernel may reach another device: no remote copies, remote signals or barrier semaphores. Data moves between devices by JAX's collectives and lax.ppermute only.
A program may use at most 64 MiB of HBM per device.

v0:
```python
import jax
import jax.numpy as jnp
from jax import lax
from jax.sharding import PartitionSpec as P

W = 256
K = 256
NS_STEPS = 4


def swapped(value, axis, apart):
    mask = 2**apart
    pairs = [(source, source ^ mask) for source in range(lax.axis_size(axis))]
    return lax.ppermute(value, axis, pairs)


def exact_dot(left_matrix, right_matrix):
    return jnp.dot(
        left_matrix,
        right_matrix,
        precision=lax.Precision.HIGHEST,
        preferred_element_type=jnp.float32,
    )


def interface_inverse(block_rows):
    slot_count, width_local, block_size = block_rows.shape
    full_block = lax.all_gather(block_rows, "sub", axis=1, tiled=True).reshape(
        block_size, block_size
    )
    row_bound = jnp.max(jnp.sum(jnp.abs(full_block), axis=1))
    iterate = jnp.eye(block_size, dtype=jnp.float32) / row_bound
    for iteration in range(NS_STEPS):
        iterate = 2.0 * iterate - exact_dot(exact_dot(full_block, iterate), iterate)
    return iterate


def shards(leaf_maps, order_one, order_two, top_data):
    width_local = leaf_maps.shape[1]
    group_index = lax.axis_index("leaf")
    member_index = lax.axis_index("sub")
    parity = group_index % 2
    is_first = parity == 0
    own_order = order_one[group_index]
    permuted = jnp.take(leaf_maps, own_order, axis=0)
    permuted = jnp.take(permuted.reshape(4, width_local, 4, W), own_order, axis=2).reshape(
        4, width_local, 4 * W
    )
    near_rows = permuted[:3]
    inner_piece = permuted[3]
    other_piece = swapped(inner_piece, "leaf", 0)
    first_piece = jnp.where(is_first, inner_piece, other_piece)
    second_piece = jnp.where(is_first, other_piece, inner_piece)
    block_one = first_piece[:, 3 * W :] + second_piece[:, 3 * W :]
    inverse_one = interface_inverse(block_one[None])
    coupling_one = near_rows[:, :, 3 * W :].reshape(3 * width_local, W)
    scaled_one = exact_dot(coupling_one, inverse_one)
    pieces = (
        lax.all_gather(first_piece[:, : 3 * W], "sub", axis=0, tiled=True),
        lax.all_gather(second_piece[:, : 3 * W], "sub", axis=0, tiled=True),
    )
    piece_rows = pieces[0].shape[0]
    joined = jnp.concatenate([pieces[0], pieces[1]], axis=1)
    coeff_part = scaled_one
    running_sum = exact_dot(coeff_part, joined)
    own_part = jnp.where(is_first, pieces[0], pieces[1]).reshape(piece_rows, 3, W)
    own_part = lax.dynamic_slice_in_dim(own_part, member_index * width_local, width_local, 2)
    kept_columns = own_part.reshape(piece_rows, 3 * width_local)
    product_one = running_sum
    right_one = kept_columns
    own_outer = near_rows[:, :, : 3 * W].reshape(3 * width_local, 3 * W)
    zero_one = jnp.zeros_like(own_outer)
    diagonal_one = jnp.where(
        is_first,
        jnp.concatenate([own_outer, zero_one], axis=1),
        jnp.concatenate([zero_one, own_outer], axis=1),
    )
    merged_one = (diagonal_one - product_one).reshape(3, width_local, 6 * W)
    node_index = group_index // 2
    node_first = node_index % 2 == 0
    node_order = order_two[node_index]
    node_rows = jnp.take(merged_one.reshape(3, width_local, 6, W), node_order, axis=2).reshape(
        3, width_local, 6 * W
    )
    position_table = jnp.sum(
        jnp.arange(6)[:, None] * (node_order[:, None] == jnp.arange(6)[None, :]).astype(jnp.int32),
        axis=0,
    )
    my_positions = jnp.take(position_table, 3 * parity + jnp.arange(3))
    slot_edges = node_order[4:6]
    slot_held = (slot_edges // 3 == parity).astype(jnp.float32)
    slot_piece = jnp.take(node_rows, slot_edges % 3, axis=0) * slot_held[:, None, None]
    node_piece = slot_piece + swapped(slot_piece, "leaf", 0)
    cousin_piece = swapped(node_piece, "leaf", 1)
    first_node = jnp.where(node_first, node_piece, cousin_piece)
    second_node = jnp.where(node_first, cousin_piece, node_piece)
    block_two = first_node[:, :, 4 * W :] + second_node[:, :, 4 * W :]
    inverse_two = interface_inverse(block_two)
    coupling_two = node_rows[:, :, 4 * W :].reshape(3 * width_local, 2 * W)
    scaled_two = exact_dot(coupling_two, inverse_two).reshape(3 * width_local, 2, W)
    top_first = 2 * (group_index % 4)
    pieces = (
        lax.all_gather(first_node[:, :, : 4 * W], "sub", axis=1, tiled=True),
        lax.all_gather(second_node[:, :, : 4 * W], "sub", axis=1, tiled=True),
    )
    piece_rows = pieces[0].shape[1]
    joined = jnp.concatenate([pieces[0], pieces[1]], axis=2)
    coeff_part = scaled_two.reshape(3 * width_local, 2 * piece_rows)
    running_sum = exact_dot(coeff_part, joined.reshape(2 * piece_rows, 8 * W))
    own_part = lax.dynamic_slice_in_dim(joined.reshape(2, piece_rows, 8, W), top_first, 2, 2)
    own_part = lax.dynamic_slice_in_dim(own_part, member_index * width_local, width_local, 3)
    kept_columns = own_part
    node_outer = node_rows[:, :, : 4 * W].reshape(3 * width_local, 4 * W)
    zero_two = jnp.zeros_like(node_outer)
    diagonal_two = jnp.where(
        node_first,
        jnp.concatenate([node_outer, zero_two], axis=1),
        jnp.concatenate([zero_two, node_outer], axis=1),
    )
    top_rows = (diagonal_two - running_sum).reshape(3, width_local, 8 * W)
    node_offset = 4 * (node_index % 2)
    buffer = jnp.zeros((8, width_local, 8 * W), jnp.float32)
    for row_slot in range(3):
        target = node_offset + my_positions[row_slot]
        marker = ((jnp.arange(8) == target) & (my_positions[row_slot] < 4)).astype(jnp.float32)
        buffer = buffer + marker[:, None, None] * top_rows[row_slot][None]
    upper_half = node_index % 2
    outgoing = lax.dynamic_slice_in_dim(buffer, 4 * (1 - upper_half), 4, 0)
    retained = lax.dynamic_slice_in_dim(buffer, 4 * upper_half, 4, 0)
    retained = retained + swapped(outgoing, "leaf", 1)
    outgoing_near = lax.dynamic_slice_in_dim(retained, 2 * (1 - parity), 2, 0)
    own_part = lax.dynamic_slice_in_dim(retained, 2 * parity, 2, 0)
    top_map = own_part + swapped(outgoing_near, "leaf", 0)
    partial_two = exact_dot(
        kept_columns.reshape(2 * W, 2 * width_local), top_data.reshape(2 * width_local, K)
    )
    partial_two = lax.psum(partial_two, "sub")
    spread = lax.dynamic_update_slice_in_dim(
        jnp.zeros((8, width_local, K), jnp.float32), top_data, top_first, 0
    )
    for bit_index in range(2):
        other_sum, other_spread = swapped((partial_two, spread), "leaf", bit_index)
        partial_two = partial_two + other_sum
        spread = spread + other_spread
    inner_two = -exact_dot(inverse_two, partial_two)
    inner_local = lax.dynamic_slice_in_dim(
        inner_two.reshape(2, W, K), member_index * width_local, width_local, 1
    )
    candidates = jnp.concatenate(
        [lax.dynamic_slice_in_dim(spread, node_offset, 4, 0), inner_local], axis=0
    )
    node_data = jnp.take(candidates, my_positions, axis=0)
    partial_one = exact_dot(right_one, node_data.reshape(3 * width_local, K))
    partial_one = lax.psum(partial_one, "sub")
    partial_one = partial_one + swapped(partial_one, "leaf", 0)
    inner_one = -exact_dot(inverse_one, partial_one)
    inner_slice = lax.dynamic_slice_in_dim(inner_one, member_index * width_local, width_local, 0)
    permuted_data = jnp.concatenate([node_data, inner_slice[None]], axis=0)
    restore = (own_order[:, None] == jnp.arange(4)[None, :]).astype(jnp.float32)
    leaf_data = jnp.zeros((4, width_local, K), jnp.float32)
    for position in range(4):
        leaf_data = leaf_data + restore[position][:, None, None] * permuted_data[position][None]
    return (top_map, leaf_data)


def solution(mesh):
    in_specs = (P("leaf", "sub", None), P(), P(), P("leaf", "sub", None))
    out_specs = (P("leaf", "sub", None), P("leaf", "sub", None))
    return jax.shard_map(shards, mesh=mesh, in_specs=in_specs, out_specs=out_specs, check_vma=False)
```

profile of v0, /device:TPU:0, one launch (start us, length us, event | category | flops | bytes accessed | tf_op | source)
XLA Modules:
  0.0 383.9 jit_solution(1197257132475756715)
XLA Ops:
  13.0 10.0 %all-gather = f32[256,256]{1,0:T(8,128)S(1)} all-gather(f32[64,256]{1,0:T(8,128)S(1)} %slice_add_fusion.1), channel_id=2, replica_groups=mesh['leaf'=8,'sub'=4] {'sub'}, dimensions={0}, use_global_device_ids=true | all-gather | bytes 327680 | tf_op jit(solution)/shard_map/all_gather | solution.py:28
  27.6 12.5 %all_gather.20 = f32[256,768]{1,0:T(8,128)S(1)} all-gather(f32[64,768]{1,0:T(8,128)S(1)} %slice.143), channel_id=1, replica_groups=mesh['leaf'=8,'sub'=4] {'sub'}, dimensions={0}, use_global_device_ids=true | all-gather | bytes 983040 | tf_op jit(solution)/shard_map/all_gather | solution.py:60
  40.0 10.2 %all_gather.19 = f32[256,768]{1,0:T(8,128)S(1)} all-gather(f32[64,768]{1,0:T(8,128)S(1)} %slice.142), channel_id=1, replica_groups=mesh['leaf'=8,'sub'=4] {'sub'}, dimensions={0}, use_global_device_ids=true | all-gather | bytes 983040 | tf_op jit(solution)/shard_map/all_gather | solution.py:59
  53.3 2.8 copy.20
  56.1 1.9 gather_fusion.3
  59.1 2.3 collective-permute-done.1
  62.4 1.6 collective-permute-start.2
  64.0 18.3 %collective-permute-done.2 = f32[2,64,1536]{2,1,0:T(8,128)} collective-permute-done((f32[2,64,1536]{2,1,0:T(8,128)}, f32[2,64,1536]{2,1,0:T(8,128)}, u32[]{:S(2)}, u32[]{:S(2)}) %collective-permute-start.2) | collective-permute-done | bytes 786464 | tf_op jit(solution)/shard_map/ppermute | solution.py:14
  85.5 1.9 slice.148
  95.5 16.9 %all-gather.5.cloned.1.call-done = f32[2,256,512]{2,1,0:T(8,128)} async-done(((f32[2,64,512]{2,1,0:T(8,128)}), f32[2,256,512]{2,1,0:T(8,128)}) %all-gather.5.cloned.1.call-update) | async-done | bytes 1048592 | tf_op jit(solution)/shard_map/all_gather | solution.py:28
  115.1 3.1 fusion.2
  118.2 1.8 fusion.7
  120.0 1.8 fusion.45
  121.8 1.8 convolution_subtract_fusion.4
  123.7 1.8 fusion.46
  125.6 1.8 convolution_subtract_fusion.3
  127.4 2.1 fusion.47
  129.5 1.9 convolution_subtract_fusion.2
  132.3 17.2 %all-gather.7.cloned.1.call-done = f32[2,256,1024]{2,1,0:T(8,128)} async-done(((f32[2,64,1024]{2,1,0:T(8,128)}), f32[2,256,1024]{2,1,0:T(8,128)}) %all-gather.7.cloned.1.call-update) | async-done | bytes 2097168 | tf_op jit(solution)/shard_map/all_gather | solution.py:103
  149.5 3.2 constant_dynamic-update-slice_fusion.1
  152.7 34.4 %all-gather.9.cloned.1.call-done = f32[2,256,1024]{2,1,0:T(8,128)} async-done(((f32[2,64,1024]{2,1,0:T(8,128)}), f32[2,256,1024]{2,1,0:T(8,128)}) %all-gather.9.cloned.1.call-update) | async-done | bytes 2097168 | tf_op jit(solution)/shard_map/all_gather | solution.py:104
  187.1 3.2 constant_dynamic-update-slice_fusion
  190.3 7.3 %copy.24 = f32[2,256,2048]{1,0,2:T(2,128)} copy(f32[2,256,2048]{2,1,0:T(8,128)} %constant_dynamic-update-slice_fusion) | data formatting | bytes 8388608 | tf_op jit(solution)/shard_map/reshape | solution.py:110
  200.2 4.7 %convolution_subtract_fusion.1 = f32[192,2048]{1,0:T(8,128)S(1)} fusion(f32[192,512]{1,0:T(8,128)S(1)} %fusion.48, f32[512,2048]{1,0:T(8,128)} %bitcast.129, f32[192,1024]{1,0:T(8,128)S(1)} %bitcast.131, pred[]{:T(512)S(6)} %eq.94), kind=kOutput, calls=%fused_computation.8 | convolution fusion | flops 2416705536 | bytes 6946817 | tf_op jit(solution)/shard_map/dot_general | solution.py:18
  205.8 39.8 %all-reduce.7.cloned.1.call-done = f32[512,256]{1,0:T(8,128)} async-done(((f32[512,256]{1,0:T(8,128)}), f32[512,256]{1,0:T(8,128)}) %all-reduce.7.cloned.1.call-update) | async-done | bytes 524304 | tf_op jit(solution)/shard_map/psum | solution.py:137
  245.6 1.8 multiply_add_fusion
  258.4 51.7 %collective-permute-done.6 = f32[8,64,256]{2,1,0:T(8,128)} collective-permute-done((f32[8,64,256]{2,1,0:T(8,128)}, f32[8,64,256]{2,1,0:T(8,128)}, u32[]{:S(2)}, u32[]{:S(2)}) %collective-permute-start.6) | collective-permute-done | bytes 524320 | tf_op jit(solution)/shard_map/ppermute | solution.py:14
  311.1 9.7 %collective-permute-done.8 = f32[512,256]{1,0:T(8,128)} collective-permute-done((f32[512,256]{1,0:T(8,128)}, f32[512,256]{1,0:T(8,128)}, u32[]{:S(2)}, u32[]{:S(2)}) %collective-permute-start.8) | collective-permute-done | bytes 524320 | tf_op jit(solution)/shard_map/ppermute | solution.py:14
  320.9 2.2 convolution_negate_fusion
  325.3 43.1 %all-reduce.9.cloned.1.call-done = f32[256,256]{1,0:T(8,128)} async-done(((f32[256,256]{1,0:T(8,128)}), f32[256,256]{1,0:T(8,128)}) %all-reduce.9.cloned.1.call-update) | async-done | bytes 262160 | tf_op jit(solution)/shard_map/psum | solution.py:154
  368.4 2.5 dynamic-slice_add_fusion
  375.1 2.3 dynamic-slice_add_fusion.1
  (135 shorter events, 46.4 us)
Async XLA Ops:
  7.2 1.2 copy-start
  7.2 105.2 %all-gather.5.cloned.1.call-start = ((), (), s32[]{:S(2)}) async-start(), calls=%async_computation | async-start | bytes 1310720 | tf_op jit(solution)/shard_map/all_gather | solution.py:28
  10.3 2.6 collective-permute-start
  26.8 23.8 %copy-start.8 = (f32[3,64,768]{2,1,0:T(8,128)S(1)}, f32[3,64,768]{2,1,0:T(8,128)}, u32[]{:S(2)}) copy-start(f32[3,64,768]{2,1,0:T(8,128)} %slice.137) | copy-start | bytes 1769476
  50.2 1.6 copy-start.5
  58.3 37.3 %copy-start.4 = (f32[3,64,1536]{2,1,0:T(8,128)}, f32[3,64,1536]{2,1,0:T(8,128)S(1)}, u32[]{:S(2)}) copy-start(f32[3,64,1536]{2,1,0:T(8,128)S(1)} %broadcast_select_fusion) | copy-start | bytes 3538948
  59.0 2.4 collective-permute-start.1
  62.4 19.9 %collective-permute-start.2 = (f32[2,64,1536]{2,1,0:T(8,128)}, f32[2,64,1536]{2,1,0:T(8,128)}, u32[]{:S(2)}, u32[]{:S(2)}) collective-permute-start(f32[2,64,1536]{2,1,0:T(8,128)} %fusion.90), channel_id=1, source_target_pairs={{0,8},{4,12},{8,0},{12,4},{16,24},{20,28},{24,16},{28,20},{1,9},{5... | collective-permute-start | bytes 2359304 | tf_op jit(solution)/shard_map/ppermute | solution.py:14
  83.8 0.9 copy-start.7
  83.8 4.5 %copy-start.9 = (f32[2,64,256]{2,1,0:T(8,128)S(1)}, f32[2,64,256]{2,1,0:T(8,128)}, u32[]{:S(2)}) copy-start(f32[2,64,256]{2,1,0:T(8,128)} %param.7) | copy-start | bytes 393220
  85.5 64.0 %all-gather.7.cloned.1.call-start = ((), (), s32[]{:S(2)}) async-start(), calls=%async_computation.1 | async-start | bytes 2621440 | tf_op jit(solution)/shard_map/all_gather | solution.py:103
  87.5 99.7 %all-gather.9.cloned.1.call-start = ((), (), s32[]{:S(2)}) async-start(), calls=%async_computation.2 | async-start | bytes 2621440 | tf_op jit(solution)/shard_map/all_gather | solution.py:104
  89.0 162.5 %collective-permute-start.5 = (f32[8,64,256]{2,1,0:T(8,128)}, f32[8,64,256]{2,1,0:T(8,128)}, u32[]{:S(2)}, u32[]{:S(2)}) collective-permute-start(f32[8,64,256]{2,1,0:T(8,128)} %constant_dynamic-update-slice_fusion.2), channel_id=1, source_target_pairs={{0,4},{4,0},{8,12},{12,8},{16,20},{20,16},{24,28},{28,24},{1,5},{5... | collective-permute-start | bytes 1572872 | tf_op jit(solution)/shard_map/ppermute | solution.py:14
  95.3 150.4 %all-reduce.7.cloned.1.call-start = ((), (), s32[]{:S(2)}) async-start(), calls=%async_computation.3 | async-start | bytes 1048576 | tf_op jit(solution)/shard_map/psum | solution.py:137
  115.1 4.9 %copy-start.2 = (f32[2,256,512]{2,1,0:T(8,128)S(1)}, f32[2,256,512]{2,1,0:T(8,128)}, u32[]{:S(2)}) copy-start(f32[2,256,512]{2,1,0:T(8,128)} %all-gather.5.cloned.1.call-done) | copy-start | bytes 3145732
  129.5 1.9 slice-start
  197.6 2.6 slice-start.1
  200.1 168.3 %all-reduce.9.cloned.1.call-start = ((), (), s32[]{:S(2)}) async-start(), calls=%async_computation.4 | async-start | bytes 524288 | tf_op jit(solution)/shard_map/psum | solution.py:154
  245.6 8.0 %collective-permute-start.7 = (f32[512,256]{1,0:T(8,128)}, f32[512,256]{1,0:T(8,128)S(1)}, u32[]{:S(2)}, u32[]{:S(2)}) collective-permute-start(f32[512,256]{1,0:T(8,128)} %all-reduce.7.cloned.1.call-done), channel_id=1, source_target_pairs={{0,4},{4,0},{8,12},{12,8},{16,20},{20,16},{24,28},{28,24},{1,5},{5... | collective-permute-start | bytes 1572872 | tf_op jit(solution)/shard_map/ppermute | solution.py:14
  247.4 2.6 copy-start.3
  247.5 6.2 %copy-start.10 = (f32[512,256]{1,0:T(8,128)S(1)}, f32[512,256]{1,0:T(8,128)}, u32[]{:S(2)}) copy-start(f32[512,256]{1,0:T(8,128)} %all-reduce.7.cloned.1.call-done) | copy-start | bytes 1572868
  247.5 8.5 %copy-start.6 = (f32[256,768]{1,0:T(8,128)S(1)}, f32[256,768]{1,0:T(8,128)}, u32[]{:S(2)}) copy-start(f32[256,768]{1,0:T(8,128)} %copy-done.5) | copy-start | bytes 2359300
  250.0 118.4 %collective-permute-start.3 = (f32[4,64,2048]{2,1,0:T(8,128)}, f32[4,64,2048]{2,1,0:T(8,128)}, u32[]{:S(2)}, u32[]{:S(2)}) collective-permute-start(f32[4,64,2048]{2,1,0:T(8,128)} %constant_dynamic-slice_fusion.3), channel_id=1, source_target_pairs={{0,8},{4,12},{8,0},{12,4},{16,24},{20,28},{24,16},{28,20},{1,9},{5... | collective-permute-start | bytes 6291464 | tf_op jit(solution)/shard_map/ppermute | solution.py:14
  253.1 57.0 %collective-permute-start.6 = (f32[8,64,256]{2,1,0:T(8,128)}, f32[8,64,256]{2,1,0:T(8,128)}, u32[]{:S(2)}, u32[]{:S(2)}) collective-permute-start(f32[8,64,256]{2,1,0:T(8,128)} %add_dynamic-update-slice_fusion), channel_id=1, source_target_pairs={{0,8},{4,12},{8,0},{12,4},{16,24},{20,28},{24,16},{28,20},{1,9},{5... | collective-permute-start | bytes 1572872 | tf_op jit(solution)/shard_map/ppermute | solution.py:14
  254.5 66.3 %collective-permute-start.8 = (f32[512,256]{1,0:T(8,128)}, f32[512,256]{1,0:T(8,128)}, u32[]{:S(2)}, u32[]{:S(2)}) collective-permute-start(f32[512,256]{1,0:T(8,128)} %add.281), channel_id=1, source_target_pairs={{0,8},{4,12},{8,0},{12,4},{16,24},{20,28},{24,16},{28,20},{1,9},{5... | collective-permute-start | bytes 1572872 | tf_op jit(solution)/shard_map/ppermute | solution.py:14
  368.4 4.1 %collective-permute-start.9 = (f32[256,256]{1,0:T(8,128)}, f32[256,256]{1,0:T(8,128)}, u32[]{:S(2)}, u32[]{:S(2)}) collective-permute-start(f32[256,256]{1,0:T(8,128)} %all-reduce.9.cloned.1.call-done), channel_id=1, source_target_pairs={{0,4},{4,0},{8,12},{12,8},{16,20},{20,16},{24,28},{28,24},{1,5},{5... | collective-permute-start | bytes 786440 | tf_op jit(solution)/shard_map/ppermute | solution.py:14
  371.9 3.1 collective-permute-start.4
  372.5 4.9 %copy-start.1 = (f32[4,64,1024]{2,1,0:T(8,128)S(1)}, f32[4,64,1024]{2,1,0:T(8,128)}, u32[]{:S(2)}) copy-start(f32[4,64,1024]{2,1,0:T(8,128)} %param.4) | copy-start | bytes 3145732
Sparse Core Ops, SparseCore 0:
  85.6 26.7 all-gather.4
  114.3 35.1 all-gather.6
  151.9 35.1 all-gather.8
  200.2 45.3 all-reduce.6
  325.3 43.0 all-reduce.8
where the time goes:
time: 385 us; the launch traced here: 384 us
  waiting for transfers between devices  234 us (61%)
  local copies, waits for them, and re-layouts  38.4 us (10%)
  matrix products  32.8 us (9%)
  blocking collectives  32.7 us (8%)
  other arithmetic  19.8 us (5%)
  between operations  19.8 us (5%)
  starting transfers between devices  6.62 us (2%)
    ppermute x10, waiting for transfers between devices, swapped(): return lax.ppermute(value, axis, pairs)  82.2 us
    psum x1, waiting for transfers between devices, shards(): partial_one = lax.psum(partial_one, 'sub')  43.1 us
    psum x1, waiting for transfers between devices, shards(): partial_two = lax.psum(partial_two, 'sub')  39.8 us
    all_gather x1, waiting for transfers between devices, shards(): lax.all_gather(second_node[:, :, :4 * W], 'sub', axis=1, tiled=True)  34.4 us
    dot_general x24, matrix products, exact_dot(): jnp.dot(left_matrix, right_matrix, precision=lax.Precision.HIGHEST, prefe...  32.8 us
    all_gather x1, waiting for transfers between devices, shards(): lax.all_gather(first_node[:, :, :4 * W], 'sub', axis=1, tiled=True)  17.2 us
    all_gather x1, waiting for transfers between devices, interface_inverse(): lax.all_gather(block_rows, 'sub', axis=1, tiled=True)  16.9 us
    all_gather x1, blocking collectives, shards(): lax.all_gather(second_piece[:, :3 * W], 'sub', axis=0, tiled=True)  12.5 us
  transfers between devices with their start and end apart: 15, of which 10 were waited for; matrix products, arithmetic and copies ran while one was open for 18% of the time, Pallas kernels for 0%

commit v1 on v0

--- a/solution.py
+++ b/solution.py
@@ -6,6 +6,33 @@
 W = 256
 K = 256
 NS_STEPS = 4
+
+
+def turn_the_digits(inp, axis_id, dim_k):
+    t_next, everything, left_arr = (
+        lax.axis_size(axis_id),
+        lax.axis_index(axis_id),
+        inp.shape[dim_k],
+    )
+    y1 = lax.dynamic_update_slice_in_dim(
+        jnp.zeros(
+            tuple((p * t_next if to_i == dim_k else p for to_i, p in enumerate(inp.shape))),
+            inp.dtype,
+        ),
+        inp,
+        everything * left_arr,
+        axis=dim_k,
+    )
+    nth = 1
+    while nth < t_next:
+        inp = lax.ppermute(
+            inp, axis_id, tuple(((to_i, (to_i + 1) % t_next) for to_i in range(t_next)))
+        )
+        y1 = lax.dynamic_update_slice_in_dim(
+            y1, inp, (everything - nth) % t_next * left_arr, axis=dim_k
+        )
+        nth += 1
+    return y1
 
 
 def swapped(value, axis, apart):
@@ -25,9 +52,7 @@
 
 def interface_inverse(block_rows):
     slot_count, width_local, block_size = block_rows.shape
-    full_block = lax.all_gather(block_rows, "sub", axis=1, tiled=True).reshape(
-        block_size, block_size
-    )
+    full_block = turn_the_digits(block_rows, "sub", 1).reshape(block_size, block_size)
     row_bound = jnp.max(jnp.sum(jnp.abs(full_block), axis=1))
     iterate = jnp.eye(block_size, dtype=jnp.float32) / row_bound
     for iteration in range(NS_STEPS):

time: 385 us -> 369 us (0.958)
  waiting for transfers between devices: 234 us -> 215 us
  starting transfers between devices: 6.62 us -> 17.3 us
  blocking collectives: 32.7 us -> 23 us
    ppermute x0 -> x6, waiting for transfers between devices: none -> 28.4 us  [turn_the_digits(): lax.ppermute(inp, axis_id, tuple(((to_i, (to_i + 1) % t_next) for to_i in...]
    all_gather x1, waiting for transfers between devices: 17.2 us -> 0.02 us  [shards(): lax.all_gather(first_node[:, :, :4 * W], 'sub', axis=1, tiled=True)]
    all_gather x1 -> x0, waiting for transfers between devices: 16.9 us -> none  [interface_inverse(): lax.all_gather(block_rows, 'sub', axis=1, tiled=True)]
    all_gather x1, waiting for transfers between devices: 34.4 us -> 21.1 us  [shards(): lax.all_gather(second_node[:, :, :4 * W], 'sub', axis=1, tiled=True)]
    ppermute x0 -> x6, starting transfers between devices: none -> 10.7 us  [turn_the_digits(): lax.ppermute(inp, axis_id, tuple(((to_i, (to_i + 1) % t_next) for to_i in...]
    all_gather x1 -> x0, blocking collectives: 10 us -> none  [interface_inverse(): lax.all_gather(block_rows, 'sub', axis=1, tiled=True)]
  transfers between devices with their start and end apart: 15 -> 20, of which waited for: 10 -> 13; matrix products, arithmetic and copies ran while one was open for 18% -> 19% of each run, Pallas kernels for 0% -> 0%
where the time goes in v1:
time: 369 us; the launch traced here: 368 us
  waiting for transfers between devices  215 us (58%)
  local copies, waits for them, and re-layouts  41.1 us (11%)
  matrix products  31.5 us (9%)
  blocking collectives  23 us (6%)
  other arithmetic  20.5 us (6%)
  between operations  19.5 us (5%)
  starting transfers between devices  17.3 us (5%)
    ppermute x10, waiting for transfers between devices, swapped(): return lax.ppermute(value, axis, pairs)  82.2 us
    psum x1, waiting for transfers between devices, shards(): partial_one = lax.psum(partial_one, 'sub')  43.1 us
    psum x1, waiting for transfers between devices, shards(): partial_two = lax.psum(partial_two, 'sub')  39.8 us
    dot_general x24, matrix products, exact_dot(): jnp.dot(left_matrix, right_matrix, precision=lax.Precision.HIGHEST, prefe...  31.5 us
    ppermute x6, waiting for transfers between devices, turn_the_digits(): lax.ppermute(inp, axis_id, tuple(((to_i, (to_i + 1) % t_next) for to_i in...  28.4 us
    all_gather x1, waiting for transfers between devices, shards(): lax.all_gather(second_node[:, :, :4 * W], 'sub', axis=1, tiled=True)  21.1 us
    all_gather x1, blocking collectives, shards(): lax.all_gather(second_piece[:, :3 * W], 'sub', axis=0, tiled=True)  12.1 us
    all_gather x1, blocking collectives, shards(): lax.all_gather(first_piece[:, :3 * W], 'sub', axis=0, tiled=True)  10.9 us
  transfers between devices with their start and end apart: 20, of which 13 were waited for; matrix products, arithmetic and copies ran while one was open for 19% of the time, Pallas kernels for 0%

profile of v1, /device:TPU:0, one launch (start us, length us, event | category | flops | bytes accessed | tf_op | source)
XLA Modules:
  0.0 367.7 jit_solution(17693430087423847383)
XLA Ops:
  13.1 2.6 collective-permute-start.1
  15.7 12.1 %all_gather.13 = f32[256,768]{1,0:T(8,128)S(1)} all-gather(f32[64,768]{1,0:T(8,128)S(1)} %slice.143), channel_id=1, replica_groups=mesh['leaf'=8,'sub'=4] {'sub'}, dimensions={0}, use_global_device_ids=true | all-gather | bytes 983040 | tf_op jit(solution)/shard_map/all_gather | solution.py:85
  27.8 10.9 %all_gather.12 = f32[256,768]{1,0:T(8,128)S(1)} all-gather(f32[64,768]{1,0:T(8,128)S(1)} %slice.142), channel_id=1, replica_groups=mesh['leaf'=8,'sub'=4] {'sub'}, dimensions={0}, use_global_device_ids=true | all-gather | bytes 983040 | tf_op jit(solution)/shard_map/all_gather | solution.py:84
  38.7 2.5 collective-permute-start.2
  41.2 2.6 collective-permute-done.2
  45.5 3.5 collective-permute-done.3
  56.6 2.8 copy.22
  59.4 1.9 gather_fusion.3
  62.4 2.3 collective-permute-done.4
  67.3 18.3 %collective-permute-done.5 = f32[2,64,1536]{2,1,0:T(8,128)} collective-permute-done((f32[2,64,1536]{2,1,0:T(8,128)}, f32[2,64,1536]{2,1,0:T(8,128)}, u32[]{:S(2)}, u32[]{:S(2)}) %collective-permute-start.5) | collective-permute-done | bytes 786464 | tf_op jit(solution)/shard_map/ppermute | solution.py:41
  85.6 2.4 broadcast_select_fusion.3
  93.9 9.6 %collective-permute-done.6 = f32[2,64,512]{2,1,0:T(8,128)} collective-permute-done((f32[2,64,512]{2,1,0:T(8,128)}, f32[2,64,512]{2,1,0:T(8,128)}, u32[]{:S(2)}, u32[]{:S(2)}) %collective-permute-start.6) | collective-permute-done | bytes 262176 | tf_op jit(solution)/shard_map/ppermute | solution.py:28
  103.5 2.6 collective-permute-start.7
  110.4 3.2 collective-permute-done.7
  118.6 9.5 %collective-permute-done.8 = f32[2,64,512]{2,1,0:T(8,128)} collective-permute-done((f32[2,64,512]{2,1,0:T(8,128)}, f32[2,64,512]{2,1,0:T(8,128)}, u32[]{:S(2)}, u32[]{:S(2)}) %collective-permute-start.8) | collective-permute-done | bytes 262176 | tf_op jit(solution)/shard_map/ppermute | solution.py:28
  136.0 1.9 convolution_subtract_fusion.4
  137.9 1.9 fusion.48
  139.7 1.8 convolution_subtract_fusion.3
  141.6 2.1 fusion.49
  143.7 1.9 convolution_subtract_fusion.2
  146.5 3.3 constant_dynamic-update-slice_fusion.6
  149.7 21.1 %all-gather.5.cloned.1.call-done = f32[2,256,1024]{2,1,0:T(8,128)} async-done(((f32[2,64,1024]{2,1,0:T(8,128)}), f32[2,256,1024]{2,1,0:T(8,128)}) %all-gather.5.cloned.1.call-update) | async-done | bytes 2097168 | tf_op jit(solution)/shard_map/all_gather | solution.py:129
  170.8 3.3 constant_dynamic-update-slice_fusion.5
  174.1 7.3 %copy.26 = f32[2,256,2048]{1,0,2:T(2,128)} copy(f32[2,256,2048]{2,1,0:T(8,128)} %constant_dynamic-update-slice_fusion.5) | data formatting | bytes 8388608 | tf_op jit(solution)/shard_map/reshape | solution.py:135
  184.0 4.7 %convolution_subtract_fusion.1 = f32[192,2048]{1,0:T(8,128)S(1)} fusion(f32[192,512]{1,0:T(8,128)S(1)} %fusion.50, f32[512,2048]{1,0:T(8,128)} %bitcast.137, f32[192,1024]{1,0:T(8,128)S(1)} %bitcast.139, pred[]{:T(512)S(6)} %eq.100), kind=kOutput, calls=%fused_computation.8 | convolution fusion | flops 2416705536 | bytes 6946817 | tf_op jit(solution)/shard_map/dot_general | solution.py:45
  189.6 39.8 %all-reduce.7.cloned.1.call-done = f32[512,256]{1,0:T(8,128)} async-done(((f32[512,256]{1,0:T(8,128)}), f32[512,256]{1,0:T(8,128)}) %all-reduce.7.cloned.1.call-update) | async-done | bytes 524304 | tf_op jit(solution)/shard_map/psum | solution.py:162
  242.3 51.7 %collective-permute-done.12 = f32[8,64,256]{2,1,0:T(8,128)} collective-permute-done((f32[8,64,256]{2,1,0:T(8,128)}, f32[8,64,256]{2,1,0:T(8,128)}, u32[]{:S(2)}, u32[]{:S(2)}) %collective-permute-start.12) | collective-permute-done | bytes 524320 | tf_op jit(solution)/shard_map/ppermute | solution.py:41
  295.0 9.7 %collective-permute-done.14 = f32[512,256]{1,0:T(8,128)} collective-permute-done((f32[512,256]{1,0:T(8,128)}, f32[512,256]{1,0:T(8,128)}, u32[]{:S(2)}, u32[]{:S(2)}) %collective-permute-start.14) | collective-permute-done | bytes 524320 | tf_op jit(solution)/shard_map/ppermute | solution.py:41
  304.7 2.2 convolution_negate_fusion
  309.1 43.1 %all-reduce.9.cloned.1.call-done = f32[256,256]{1,0:T(8,128)} async-done(((f32[256,256]{1,0:T(8,128)}), f32[256,256]{1,0:T(8,128)}) %all-reduce.9.cloned.1.call-update) | async-done | bytes 262160 | tf_op jit(solution)/shard_map/psum | solution.py:179
  352.2 2.5 dynamic-slice_add_fusion
  358.9 2.3 dynamic-slice_add_fusion.1
  (151 shorter events, 61.1 us)
Async XLA Ops:
  7.2 139.3 %all-gather.3.cloned.1.call-start = ((), (), s32[]{:S(2)}) async-start(), calls=%async_computation | async-start | bytes 2621440 | tf_op jit(solution)/shard_map/all_gather | solution.py:128
  10.3 2.7 collective-permute-start
  13.1 25.5 %collective-permute-start.1 = (f32[1,64,256]{2,1,0:T(8,128)S(1)}, f32[1,64,256]{2,1,0:T(8,128)S(1)}, u32[]{:S(2)}, u32[]{:S(2)}) collective-permute-start(f32[1,64,256]{2,1,0:T(8,128)S(1)} %get-tuple-element.13), channel_id=1, source_target_pairs={{0,1},{1,2},{2,3},{3,0},{4,5},{5,6},{6,7},{7,4},{8,9},{9,10},{10,1... | collective-permute-start | bytes 196616 | tf_op jit(solution)/shard_map/ppermute | solution.py:28
  38.7 15.2 %copy-start.4 = (f32[256,768]{1,0:T(8,128)}, f32[256,768]{1,0:T(8,128)S(1)}, u32[]{:S(2)}) copy-start(f32[256,768]{1,0:T(8,128)S(1)} %all_gather.12) | copy-start | bytes 2359300
  38.7 5.2 %collective-permute-start.2 = (f32[1,64,256]{2,1,0:T(8,128)S(1)}, f32[1,64,256]{2,1,0:T(8,128)S(1)}, u32[]{:S(2)}, u32[]{:S(2)}) collective-permute-start(f32[1,64,256]{2,1,0:T(8,128)S(1)} %collective-permute-done.1), channel_id=1, source_target_pairs={{0,1},{1,2},{2,3},{3,0},{4,5},{5,6},{6,7},{7,4},{8,9},{9,10},{10,1... | collective-permute-start | bytes 196616 | tf_op jit(solution)/shard_map/ppermute | solution.py:28
  43.8 5.2 %collective-permute-start.3 = (f32[1,64,256]{2,1,0:T(8,128)S(1)}, f32[1,64,256]{2,1,0:T(8,128)S(1)}, u32[]{:S(2)}, u32[]{:S(2)}) collective-permute-start(f32[1,64,256]{2,1,0:T(8,128)S(1)} %collective-permute-done.2), channel_id=1, source_target_pairs={{0,1},{1,2},{2,3},{3,0},{4,5},{5,6},{6,7},{7,4},{8,9},{9,10},{10,1... | collective-permute-start | bytes 196616 | tf_op jit(solution)/shard_map/ppermute | solution.py:28
  52.0 1.9 copy-start.8
  61.6 52.7 %copy-start.3 = (f32[3,64,1536]{2,1,0:T(8,128)}, f32[3,64,1536]{2,1,0:T(8,128)S(1)}, u32[]{:S(2)}) copy-start(f32[3,64,1536]{2,1,0:T(8,128)S(1)} %broadcast_select_fusion) | copy-start | bytes 3538948
  62.3 2.4 collective-permute-start.4
  65.7 19.9 %collective-permute-start.5 = (f32[2,64,1536]{2,1,0:T(8,128)}, f32[2,64,1536]{2,1,0:T(8,128)}, u32[]{:S(2)}, u32[]{:S(2)}) collective-permute-start(f32[2,64,1536]{2,1,0:T(8,128)} %fusion.92), channel_id=1, source_target_pairs={{0,8},{4,12},{8,0},{12,4},{16,24},{20,28},{24,16},{28,20},{1,9},{5... | collective-permute-start | bytes 2359304 | tf_op jit(solution)/shard_map/ppermute | solution.py:41
  67.3 22.5 %copy-start.9 = (f32[2,64,256]{2,1,0:T(8,128)S(1)}, f32[2,64,256]{2,1,0:T(8,128)}, u32[]{:S(2)}) copy-start(f32[2,64,256]{2,1,0:T(8,128)} %param.7) | copy-start | bytes 393220
  88.0 2.5 copy-start.7
  88.9 81.9 %all-gather.5.cloned.1.call-start = ((), (), s32[]{:S(2)}) async-start(), calls=%async_computation.1 | async-start | bytes 2621440 | tf_op jit(solution)/shard_map/all_gather | solution.py:129
  90.5 144.9 %collective-permute-start.11 = (f32[8,64,256]{2,1,0:T(8,128)}, f32[8,64,256]{2,1,0:T(8,128)}, u32[]{:S(2)}, u32[]{:S(2)}) collective-permute-start(f32[8,64,256]{2,1,0:T(8,128)} %constant_dynamic-update-slice_fusion), channel_id=1, source_target_pairs={{0,4},{4,0},{8,12},{12,8},{16,20},{20,16},{24,28},{28,24},{1,5},{5... | collective-permute-start | bytes 1572872 | tf_op jit(solution)/shard_map/ppermute | solution.py:41
  92.4 11.1 %collective-permute-start.6 = (f32[2,64,512]{2,1,0:T(8,128)}, f32[2,64,512]{2,1,0:T(8,128)}, u32[]{:S(2)}, u32[]{:S(2)}) collective-permute-start(f32[2,64,512]{2,1,0:T(8,128)} %get-tuple-element.5), channel_id=1, source_target_pairs={{0,1},{1,2},{2,3},{3,0},{4,5},{5,6},{6,7},{7,4},{8,9},{9,10},{10,1... | collective-permute-start | bytes 786440 | tf_op jit(solution)/shard_map/ppermute | solution.py:28
  103.5 10.1 %collective-permute-start.7 = (f32[2,64,512]{2,1,0:T(8,128)}, f32[2,64,512]{2,1,0:T(8,128)}, u32[]{:S(2)}, u32[]{:S(2)}) collective-permute-start(f32[2,64,512]{2,1,0:T(8,128)} %collective-permute-done.6), channel_id=1, source_target_pairs={{0,1},{1,2},{2,3},{3,0},{4,5},{5,6},{6,7},{7,4},{8,9},{9,10},{10,1... | collective-permute-start | bytes 786440 | tf_op jit(solution)/shard_map/ppermute | solution.py:28
  113.6 14.6 %collective-permute-start.8 = (f32[2,64,512]{2,1,0:T(8,128)}, f32[2,64,512]{2,1,0:T(8,128)}, u32[]{:S(2)}, u32[]{:S(2)}) collective-permute-start(f32[2,64,512]{2,1,0:T(8,128)} %collective-permute-done.7), channel_id=1, source_target_pairs={{0,1},{1,2},{2,3},{3,0},{4,5},{5,6},{6,7},{7,4},{8,9},{9,10},{10,1... | collective-permute-start | bytes 786440 | tf_op jit(solution)/shard_map/ppermute | solution.py:28
  114.2 1.4 copy-start.6
  116.4 113.0 %all-reduce.7.cloned.1.call-start = ((), (), s32[]{:S(2)}) async-start(), calls=%async_computation.2 | async-start | bytes 1048576 | tf_op jit(solution)/shard_map/psum | solution.py:162
  143.7 1.9 slice-start
  181.4 2.6 slice-start.1
  183.9 168.3 %all-reduce.9.cloned.1.call-start = ((), (), s32[]{:S(2)}) async-start(), calls=%async_computation.3 | async-start | bytes 524288 | tf_op jit(solution)/shard_map/psum | solution.py:179
  229.5 8.0 %collective-permute-start.13 = (f32[512,256]{1,0:T(8,128)}, f32[512,256]{1,0:T(8,128)S(1)}, u32[]{:S(2)}, u32[]{:S(2)}) collective-permute-start(f32[512,256]{1,0:T(8,128)} %all-reduce.7.cloned.1.call-done), channel_id=1, source_target_pairs={{0,4},{4,0},{8,12},{12,8},{16,20},{20,16},{24,28},{28,24},{1,5},{5... | collective-permute-start | bytes 1572872 | tf_op jit(solution)/shard_map/ppermute | solution.py:41
  231.3 2.6 copy-start.2
  231.3 6.2 %copy-start.10 = (f32[512,256]{1,0:T(8,128)S(1)}, f32[512,256]{1,0:T(8,128)}, u32[]{:S(2)}) copy-start(f32[512,256]{1,0:T(8,128)} %all-reduce.7.cloned.1.call-done) | copy-start | bytes 1572868
  231.3 8.6 %copy-start.5 = (f32[256,768]{1,0:T(8,128)S(1)}, f32[256,768]{1,0:T(8,128)}, u32[]{:S(2)}) copy-start(f32[256,768]{1,0:T(8,128)} %copy-done.4) | copy-start | bytes 2359300
  233.9 118.4 %collective-permute-start.9 = (f32[4,64,2048]{2,1,0:T(8,128)}, f32[4,64,2048]{2,1,0:T(8,128)}, u32[]{:S(2)}, u32[]{:S(2)}) collective-permute-start(f32[4,64,2048]{2,1,0:T(8,128)} %constant_dynamic-slice_fusion.3), channel_id=1, source_target_pairs={{0,8},{4,12},{8,0},{12,4},{16,24},{20,28},{24,16},{28,20},{1,9},{5... | collective-permute-start | bytes 6291464 | tf_op jit(solution)/shard_map/ppermute | solution.py:41
  236.9 57.0 %collective-permute-start.12 = (f32[8,64,256]{2,1,0:T(8,128)}, f32[8,64,256]{2,1,0:T(8,128)}, u32[]{:S(2)}, u32[]{:S(2)}) collective-permute-start(f32[8,64,256]{2,1,0:T(8,128)} %add_dynamic-update-slice_fusion), channel_id=1, source_target_pairs={{0,8},{4,12},{8,0},{12,4},{16,24},{20,28},{24,16},{28,20},{1,9},{5... | collective-permute-start | bytes 1572872 | tf_op jit(solution)/shard_map/ppermute | solution.py:41
  238.3 66.3 %collective-permute-start.14 = (f32[512,256]{1,0:T(8,128)}, f32[512,256]{1,0:T(8,128)}, u32[]{:S(2)}, u32[]{:S(2)}) collective-permute-start(f32[512,256]{1,0:T(8,128)} %add.316), channel_id=1, source_target_pairs={{0,8},{4,12},{8,0},{12,4},{16,24},{20,28},{24,16},{28,20},{1,9},{5... | collective-permute-start | bytes 1572872 | tf_op jit(solution)/shard_map/ppermute | solution.py:41
  352.2 4.1 %collective-permute-start.15 = (f32[256,256]{1,0:T(8,128)}, f32[256,256]{1,0:T(8,128)}, u32[]{:S(2)}, u32[]{:S(2)}) collective-permute-start(f32[256,256]{1,0:T(8,128)} %all-reduce.9.cloned.1.call-done), channel_id=1, source_target_pairs={{0,4},{4,0},{8,12},{12,8},{16,20},{20,16},{24,28},{28,24},{1,5},{5... | collective-permute-start | bytes 786440 | tf_op jit(solution)/shard_map/ppermute | solution.py:41
  355.8 3.1 collective-permute-start.10
  356.3 4.9 %copy-start.1 = (f32[4,64,1024]{2,1,0:T(8,128)S(1)}, f32[4,64,1024]{2,1,0:T(8,128)}, u32[]{:S(2)}) copy-start(f32[4,64,1024]{2,1,0:T(8,128)} %param.4) | copy-start | bytes 3145732
  (1 other events, 1.2 us)
Sparse Core Ops, SparseCore 0:
  89.0 44.7 all-gather.2
  136.3 34.5 all-gather.4
  184.0 45.3 all-reduce.6
  309.1 43.0 all-reduce.8
